TPU v7x, 32 devices: a whole 2x2x4 slice. The times are simulated.
32 devices in a mesh: rad: 8 (over z, y), ell: 4 (over x, core).
Axes of the slice: x: 2, y: 2, z: 4, core: 2. Of those that a mesh axis runs over, the one named last changes fastest.
Arguments:
- field: bfloat16 [512, 128, 512], P('rad', 'ell'), may hold values from -6 to 6
- projection: bfloat16 [512, 128, 256], P('rad', 'ell'), may hold values from -0.375 to 0.375
- ell_ids: int32 [128], P('ell'), may hold values from 0 to 255, as said below
Outputs:
- share: float32 [128, 256], P('ell', 'rad')
- crest: float32 [128, 256], P('ell', 'rad')
Inputs may be any that keep to these rules, and one draw needn't show every extreme that they name: `ell_ids`: distinct and ascending.
All inputs are finite; a program needn't handle non-finite values.
Results may differ from a plain program's by a relative error of at most 0.0003.
Values may be sent and summed in bfloat16 or wider, within the bound.
A program may use at most 64 MiB of HBM per device.

v0:
```python
import jax
import jax.numpy as jnp
from jax import lax
from jax.sharding import PartitionSpec as P


def per_device(field, projection, ell_ids):
    exchanged = lax.all_to_all(field, "rad", split_axis=2, concat_axis=0, tiled=True)
    slot_share = exchanged.shape[2]
    coef = jnp.einsum(
        "rem,ren->emn",
        exchanged,
        lax.all_gather(projection, "rad", axis=0, tiled=True),
        preferred_element_type=jnp.float32,
    )
    slots = lax.axis_index("rad") * slot_share + jnp.arange(slot_share, dtype=jnp.int32)
    valid = (slots[None, :] < 2 * ell_ids[:, None] + 1).astype(jnp.float32)
    energy_part = jnp.sum(valid[:, :, None] * coef * coef, axis=1)
    peak_part = jnp.max(valid[:, :, None] * jnp.abs(coef), axis=1)
    energy_all, peak_all = (
        lax.all_to_all(energy_part[None], "rad", split_axis=2, concat_axis=0, tiled=True),
        lax.all_to_all(peak_part[None], "rad", split_axis=2, concat_axis=0, tiled=True),
    )
    energy = jnp.sum(energy_all, axis=0)
    peak = jnp.max(peak_all, axis=0)
    local_sum = jnp.sum(energy, axis=0)
    local_top = jnp.max(peak, axis=0)
    column = lax.psum(local_sum, "ell")
    top = lax.pmax(local_top, "ell")
    column = column + 1e-06
    top = top + 1e-06
    total_ells = ell_ids.shape[0] * lax.axis_size("ell")
    share = total_ells * energy / column[None, :]
    crest = peak / top[None, :]
    return (share, crest)


def solution(mesh):
    in_specs = (P("rad", "ell", None), P("rad", "ell", None), P("ell"))
    out_specs = (P("ell", "rad"), P("ell", "rad"))
    return jax.shard_map(
        per_device, mesh=mesh, in_specs=in_specs, out_specs=out_specs, check_vma=False
    )
```

profile of v0, /device:TPU:0, one launch (start us, length us, event | category | flops | bytes accessed | tf_op | source)
XLA Modules:
  0.0 218.3 jit_solution(14163633866488096663)
XLA Ops:
  7.2 2.9 %copy.19 = bf16[64,32,256]{2,0,1:T(8,128)(2,1)} copy(bf16[64,32,256]{2,1,0:T(8,128)(2,1)} %param.4) | data formatting | bytes 2097152 | tf_op args[1]
  10.2 7.8 %copy.17 = bf16[64,32,512]{0,1,2:T(8,128)(2,1)} copy(bf16[64,32,512]{2,1,0:T(8,128)(2,1)S(1)} %copy-done) | data formatting | bytes 4194304 | tf_op args[0]
  18.0 7.7 %reshape.45 = bf16[8,2,65536]{2,1,0:T(2,128)(2,1)} reshape(bf16[512,32,64]{2,1,0:T(8,128)(2,1)} %bitcast.22) | data formatting | bytes 4194304
  25.7 7.5 %all-to-all-start = ((bf16[8,2,65536]{2,1,0:T(2,128)(2,1)}), bf16[8,2,65536]{2,1,0:T(2,128)(2,1)S(1)}, u32[]{:S(2)}, u32[]{:S(2)}) async-start(bf16[8,2,65536]{2,1,0:T(2,128)(2,1)} %reshape.45), calls=%async_computation | async-start | bytes 4194304 | tf_op jit(solution)/shard_map/all_to_all | solution.py:8
  33.2 87.4 %all-to-all-done = bf16[8,2,65536]{2,1,0:T(2,128)(2,1)S(1)} async-done(((bf16[8,2,65536]{2,1,0:T(2,128)(2,1)}), bf16[8,2,65536]{2,1,0:T(2,128)(2,1)S(1)}, u32[]{:S(2)}, u32[]{:S(2)}) %all-to-all-start) | async-done | bytes 2097184 | tf_op jit(solution)/shard_map/all_to_all | solution.py:8
  120.7 5.0 %reshape.46 = bf16[512,32,64]{2,1,0:T(8,128)(2,1)} reshape(bf16[8,2,65536]{2,1,0:T(2,128)(2,1)S(1)} %all-to-all-done) | data formatting | bytes 4194304
  125.7 6.8 %copy.25 = bf16[64,32,8,64]{0,2,3,1:T(8,128)(2,1)} copy(bf16[64,32,8,64]{0,1,3,2:T(8,128)(2,1)} %bitcast.23) | data formatting | bytes 4194304 | tf_op jit(solution)/shard_map/all_to_all | solution.py:8
  132.5 5.4 %all_to_all.34 = bf16[512,32,64]{0,2,1:T(8,128)(2,1)S(1)} reshape(bf16[8,64,32,64]{1,0,3,2:T(8,128)(2,1)} %bitcast.24) | data formatting | bytes 4194304 | tf_op jit(solution)/shard_map/all_to_all | solution.py:8
  137.9 35.0 %all-gather.2.cloned.1.call-done = bf16[512,32,256]{2,0,1:T(8,128)(2,1)} async-done(((bf16[64,32,256]{2,0,1:T(8,128)(2,1)}), bf16[512,32,256]{2,0,1:T(8,128)(2,1)}) %all-gather.2.cloned.1.call-update) | async-done | bytes 8388624 | tf_op jit(solution)/shard_map/all_gather | solution.py:13
  172.9 4.9 %multiply_reduce_fusion = (f32[32,256]{1,0:T(8,128)S(1)}, f32[32,256]{1,0:T(8,128)S(1)}) fusion(f32[32,64]{1,0:T(8,128)S(1)} %compare_convert_fusion, bf16[512,32,64]{0,2,1:T(8,128)(2,1)S(1)} %all_to_all.34, bf16[512,32,256]{2,0,1:T(8,128)(2,1)} %all-gather.2.cloned.1.call-done), kind=kOutput, calls=%fused_computation.3 | convolution fusion | flops 540000256 | bytes 10559488 | tf_op jit(solution)/shard_map/rem,ren->emn/dot_general | solution.py:10
  178.4 1.0 reduce.18
  179.4 0.7 reshape.49
  180.1 3.3 %all-to-all-start.2 = ((f32[8,1,1024]{2,1,0:T(1,128)}), f32[8,1,1024]{2,1,0:T(1,128)S(1)}, u32[]{:S(2)}, u32[]{:S(2)}) async-start(f32[8,1,1024]{2,1,0:T(1,128)} %reshape.49), calls=%async_computation.2 | async-start | bytes 65536 | tf_op jit(solution)/shard_map/all_to_all | solution.py:22
  183.6 1.0 reduce.16
  184.6 0.7 reshape.47
  185.3 4.8 %all-to-all-done.2 = f32[8,1,1024]{2,1,0:T(1,128)S(1)} async-done(((f32[8,1,1024]{2,1,0:T(1,128)}), f32[8,1,1024]{2,1,0:T(1,128)S(1)}, u32[]{:S(2)}, u32[]{:S(2)}) %all-to-all-start.2) | async-done | bytes 32800 | tf_op jit(solution)/shard_map/all_to_all | solution.py:22
  190.1 3.3 %all-to-all-start.1 = ((f32[8,1,1024]{2,1,0:T(1,128)}), f32[8,1,1024]{2,1,0:T(1,128)S(1)}, u32[]{:S(2)}, u32[]{:S(2)}) async-start(f32[8,1,1024]{2,1,0:T(1,128)} %reshape.47), calls=%async_computation.1 | async-start | bytes 65536 | tf_op jit(solution)/shard_map/all_to_all | solution.py:21
  193.4 0.7 reduce.19
  194.4 1.0 bitcast_reduce_fusion
  195.6 6.0 %pmax.7 = f32[32]{0:T(128)S(1)} all-reduce(f32[32]{0:T(128)S(1)} %reduce_max.38), channel_id=1, replica_groups=mesh['rad'=8,'ell'=4] {'ell'}, use_global_device_ids=true, to_apply=%region_9.10 | all-reduce | flops 32 | bytes 256 | tf_op jit(solution)/shard_map/pmax | solution.py:29
  201.6 0.7 copy.23
  202.3 0.7 reduce.17
  203.2 1.0 bitcast_reduce_fusion.1
  204.4 6.3 %psum.7 = f32[32]{0:T(128)S(1)} all-reduce(f32[32]{0:T(128)S(1)} %reduce_sum.38), channel_id=1, replica_groups=mesh['rad'=8,'ell'=4] {'ell'}, use_global_device_ids=true, to_apply=%region_4.0 | all-reduce | flops 32 | bytes 256 | tf_op jit(solution)/shard_map/psum | solution.py:28
  (26 shorter events, 2.4 us)
Async XLA Ops:
  7.2 3.0 %copy-start = (bf16[64,32,512]{2,1,0:T(8,128)(2,1)S(1)}, bf16[64,32,512]{2,1,0:T(8,128)(2,1)}, u32[]{:S(2)}) copy-start(bf16[64,32,512]{2,1,0:T(8,128)(2,1)} %param.3) | copy-start | bytes 6291460
  7.2 165.7 %all-gather.2.cloned.1.call-start = ((), (), s32[]{:S(2)}) async-start(), calls=%async_computation.3 | async-start | bytes 9437184 | tf_op jit(solution)/shard_map/all_gather | solution.py:13
  25.7 7.5 %copy-start.1 = (s32[32]{0:T(128)S(1)}, s32[32]{0:T(128)}, u32[]{:S(2)}) copy-start(s32[32]{0:T(128)} %param.5) | copy-start | bytes 388
  25.7 95.0 %all-to-all-start = ((bf16[8,2,65536]{2,1,0:T(2,128)(2,1)}), bf16[8,2,65536]{2,1,0:T(2,128)(2,1)S(1)}, u32[]{:S(2)}, u32[]{:S(2)}) async-start(bf16[8,2,65536]{2,1,0:T(2,128)(2,1)} %reshape.45), calls=%async_computation | async-start | bytes 4194304 | tf_op jit(solution)/shard_map/all_to_all | solution.py:8
  180.1 10.0 %all-to-all-start.2 = ((f32[8,1,1024]{2,1,0:T(1,128)}), f32[8,1,1024]{2,1,0:T(1,128)S(1)}, u32[]{:S(2)}, u32[]{:S(2)}) async-start(f32[8,1,1024]{2,1,0:T(1,128)} %reshape.49), calls=%async_computation.2 | async-start | bytes 65536 | tf_op jit(solution)/shard_map/all_to_all | solution.py:22
  190.1 12.2 %all-to-all-start.1 = ((f32[8,1,1024]{2,1,0:T(1,128)}), f32[8,1,1024]{2,1,0:T(1,128)S(1)}, u32[]{:S(2)}, u32[]{:S(2)}) async-start(f32[8,1,1024]{2,1,0:T(1,128)} %reshape.47), calls=%async_computation.1 | async-start | bytes 65536 | tf_op jit(solution)/shard_map/all_to_all | solution.py:21
Sparse Core Ops, SparseCore 0:
  10.3 162.5 all-gather.1
where the time goes:
time: 219 us; the launch traced here: 218 us
  waiting for transfers between devices  127 us (58%)
  local copies, waits for them, and re-layouts  39.8 us (18%)
  starting transfers between devices  14.2 us (6%)
  between operations  14.2 us (6%)
  blocking collectives  12.3 us (6%)
  other arithmetic  5.77 us (3%)
  matrix products  4.92 us (2%)
    all_to_all x1, waiting for transfers between devices, per_device(): lax.all_to_all(field, 'rad', split_axis=2, concat_axis=0, tiled=True)  87.4 us
    all_gather x1, waiting for transfers between devices, per_device(): lax.all_gather(projection, 'rad', axis=0, tiled=True)  35 us
    unnamed x15, local copies, waits for them, and re-layouts  27.2 us
    all_to_all x2, local copies, waits for them, and re-layouts, per_device(): lax.all_to_all(field, 'rad', split_axis=2, concat_axis=0, tiled=True)  12.2 us
    all_to_all x1, starting transfers between devices, per_device(): lax.all_to_all(field, 'rad', split_axis=2, concat_axis=0, tiled=True)  7.47 us
    psum x1, blocking collectives, per_device(): column = lax.psum(local_sum, 'ell')  6.3 us
    pmax x1, blocking collectives, per_device(): top = lax.pmax(local_top, 'ell')  5.96 us
    dot_general x1, matrix products, per_device(): jnp.einsum('rem,ren->emn', exchanged, lax.all_gather(projection, 'rad', a...  4.92 us
  transfers between devices with their start and end apart: 4, of which 3 were waited for; matrix products, arithmetic and copies ran while one was open for 15% of the time, Pallas kernels for 0%

commit v1 on v0

--- a/solution.py
+++ b/solution.py
@@ -1,10 +1,162 @@
+import functools
+
 import jax
 import jax.numpy as jnp
 from jax import lax
+from jax.experimental import pallas as pl
+from jax.experimental.pallas import tpu as pltpu
 from jax.sharding import PartitionSpec as P
 
+MESH = pl.DeviceIdType.MESH
 
-def per_device(field, projection, ell_ids):
+
+def flipped(me, step, n):
+    peer, bit = 0, 1
+    while bit < n:
+        b = (me // bit) % 2
+        peer = peer + bit * ((1 - b) if step & bit else b)
+        bit *= 2
+    return peer
+
+
+def project_kernel(n, n_ell, own, depth, m_size, n_size, ell_ref, fp_ref, energy_ref, peak_ref, total_ref,
+                   held, mine, stats, mine2, totals,
+                   send_sem, recv_sem, local_sem, send2, recv2, send3, recv3):
+    me = lax.axis_index("rad")
+    my_ell = lax.axis_index("ell")
+    barrier = pltpu.get_barrier_semaphore()
+    for s in range(1, n):
+        pl.semaphore_signal(barrier, inc=1, device_id={"rad": flipped(me, s, n)}, device_id_type=MESH)
+    for s in range(1, n_ell):
+        pl.semaphore_signal(barrier, inc=1, device_id={"ell": lax.rem(my_ell + s, n_ell)}, device_id_type=MESH)
+
+    rows = pl.ds(pl.multiple_of(me * depth, depth), depth)
+    locals_ = []
+    for e in range(own):
+        copy = pltpu.make_async_copy(fp_ref.at[me * own + e], held.at[e, rows], local_sem.at[e])
+        copy.start()
+        locals_.append(copy)
+    pl.semaphore_wait(barrier, n - 1 + n_ell - 1)
+
+    sends = []
+    for e in range(own):
+        chunk = []
+        for s in range(n - 1, 0, -1):
+            peer = flipped(me, s, n)
+            copy = pltpu.make_async_remote_copy(
+                src_ref=fp_ref.at[peer * own + e],
+                dst_ref=held.at[e, rows],
+                send_sem=send_sem.at[e, s],
+                recv_sem=recv_sem.at[e, s],
+                device_id={"rad": peer},
+                device_id_type=MESH,
+            )
+            copy.start()
+            chunk.append(copy)
+        sends.append(chunk)
+
+    slots = lax.broadcasted_iota(jnp.int32, (m_size, n_size), 0)
+    for e in range(own):
+        locals_[e].wait()
+        for copy in sends[e]:
+            copy.wait_recv()
+        coef = lax.dot_general(
+            held[e, :, :m_size], held[e, :, m_size:], (((0,), (0,)), ((), ())),
+            preferred_element_type=jnp.float32,
+        )
+        valid = slots < 2 * ell_ref[me * own + e] + 1
+        coef = jnp.where(valid, coef, 0.0)
+        mine[e : e + 1, :] = jnp.sum(coef * coef, axis=0, keepdims=True)
+        mine[own + e : own + e + 1, :] = jnp.max(jnp.abs(coef), axis=0, keepdims=True)
+
+    copies = []
+    for s in range(n - 1, 0, -1):
+        copy = pltpu.make_async_remote_copy(
+            src_ref=mine, dst_ref=stats.at[me], send_sem=send2.at[s], recv_sem=recv2.at[s],
+            device_id={"rad": flipped(me, s, n)}, device_id_type=MESH,
+        )
+        copy.start()
+        copies.append(copy)
+    stats[me] = mine[...]
+    for copy in copies:
+        copy.wait_recv()
+    every = stats[...]
+    column = jnp.zeros((1, n_size), jnp.float32)
+    top = jnp.zeros((1, n_size), jnp.float32)
+    for s in range(n):
+        energy_ref[s * own : (s + 1) * own, :] = every[s, :own]
+        peak_ref[s * own : (s + 1) * own, :] = every[s, own:]
+        column = column + jnp.sum(every[s, :own], axis=0, keepdims=True)
+        top = jnp.maximum(top, jnp.max(every[s, own:], axis=0, keepdims=True))
+    mine2[0:1, :] = column
+    mine2[1:2, :] = top
+    others = []
+    for s in range(1, n_ell):
+        copy = pltpu.make_async_remote_copy(
+            src_ref=mine2, dst_ref=totals.at[my_ell], send_sem=send3.at[s], recv_sem=recv3.at[s],
+            device_id={"ell": lax.rem(my_ell + s, n_ell)}, device_id_type=MESH,
+        )
+        copy.start()
+        others.append(copy)
+    totals[my_ell] = mine2[...]
+    for copy in others:
+        copy.wait_recv()
+    both = totals[...]
+    column = both[0, 0:1]
+    top = both[0, 1:2]
+    for s in range(1, n_ell):
+        column = column + both[s, 0:1]
+        top = jnp.maximum(top, both[s, 1:2])
+    total_ref[0:1, :] = column
+    total_ref[1:2, :] = top
+    for chunk in sends:
+        for copy in chunk:
+            copy.wait_send()
+    for copy in copies + others:
+        copy.wait_send()
+
+
+def by_ells(field, projection, ell_ids):
+    n, n_ell = lax.axis_size("rad"), lax.axis_size("ell")
+    depth, ells, m_size = field.shape
+    n_size = projection.shape[2]
+    own = ells // n
+    fp = jnp.transpose(jnp.concatenate([field, projection], axis=2), (1, 0, 2))
+    vmem = pl.BlockSpec(memory_space=pltpu.VMEM)
+    energy, peak, total = pl.pallas_call(
+        functools.partial(project_kernel, n, n_ell, own, depth, m_size, n_size),
+        out_shape=(
+            jax.ShapeDtypeStruct((ells, n_size), jnp.float32),
+            jax.ShapeDtypeStruct((ells, n_size), jnp.float32),
+            jax.ShapeDtypeStruct((2, n_size), jnp.float32),
+        ),
+        in_specs=[pl.BlockSpec(memory_space=pltpu.SMEM), pl.BlockSpec(memory_space=pl.ANY)],
+        out_specs=(vmem, vmem, vmem),
+        scratch_shapes=[
+            pltpu.VMEM((own, n * depth, m_size + n_size), jnp.bfloat16),
+            pltpu.VMEM((2 * own, n_size), jnp.float32),
+            pltpu.VMEM((n, 2 * own, n_size), jnp.float32),
+            pltpu.VMEM((2, n_size), jnp.float32),
+            pltpu.VMEM((n_ell, 2, n_size), jnp.float32),
+            pltpu.SemaphoreType.DMA((own, n)),
+            pltpu.SemaphoreType.DMA((own, n)),
+            pltpu.SemaphoreType.DMA((own,)),
+            pltpu.SemaphoreType.DMA((n,)),
+            pltpu.SemaphoreType.DMA((n,)),
+            pltpu.SemaphoreType.DMA((n_ell,)),
+            pltpu.SemaphoreType.DMA((n_ell,)),
+        ],
+        compiler_params=pltpu.CompilerParams(collective_id=0, has_side_effects=True),
+    )(ell_ids, fp)
+    width = n_size // n
+    start = lax.axis_index("rad") * width
+    energy, peak, total = (lax.dynamic_slice_in_dim(a, start, width, axis=1) for a in (energy, peak, total))
+    share = (ells * n_ell) * energy / (total[0:1] + 1e-06)
+    crest = peak / (total[1:2] + 1e-06)
+    return share, crest
+
+
+def by_slots(field, projection, ell_ids):
     exchanged = lax.all_to_all(field, "rad", split_axis=2, concat_axis=0, tiled=True)
     slot_share = exchanged.shape[2]
     coef = jnp.einsum(
@@ -23,16 +175,20 @@
     )
     energy = jnp.sum(energy_all, axis=0)
     peak = jnp.max(peak_all, axis=0)
-    local_sum = jnp.sum(energy, axis=0)
-    local_top = jnp.max(peak, axis=0)
-    column = lax.psum(local_sum, "ell")
-    top = lax.pmax(local_top, "ell")
-    column = column + 1e-06
-    top = top + 1e-06
+    column = lax.psum(jnp.sum(energy, axis=0), "ell") + 1e-06
+    top = lax.pmax(jnp.max(peak, axis=0), "ell") + 1e-06
     total_ells = ell_ids.shape[0] * lax.axis_size("ell")
     share = total_ells * energy / column[None, :]
     crest = peak / top[None, :]
     return (share, crest)
+
+
+def per_device(field, projection, ell_ids):
+    n = lax.axis_size("rad")
+    depth, ells, _ = field.shape
+    if ells % n == 0 and n & (n - 1) == 0 and depth % 16 == 0:
+        return by_ells(field, projection, ell_ids)
+    return by_slots(field, projection, ell_ids)
 
 
 def solution(mesh):

time: 219 us -> 93 us (0.42)
  waiting for transfers between devices: 127 us -> 0 us
  Pallas kernels: 0 us -> 84.9 us
  local copies, waits for them, and re-layouts: 39.8 us -> 3.83 us
  starting transfers between devices: 14.2 us -> 0 us
  between operations: 14.2 us -> 0.66 us
  blocking collectives: 12.3 us -> 0 us
  matrix products: 4.92 us -> 0 us
  other arithmetic: 5.77 us -> 3.35 us
    all_to_all x3 -> x0, waiting for transfers between devices: 92.2 us -> none  [the longest x1 87.4 us: per_device(): lax.all_to_all(field, 'rad', split_axis=2, concat_axis=0, tiled=True)]
    pallas_call x0 -> x1, Pallas kernels: none -> 84.9 us  [by_ells(): pl.pallas_call(functools.partial(project_kernel, n, n_ell, own, depth, m_...]
    all_gather x1 -> x0, waiting for transfers between devices: 35 us -> none  [per_device(): lax.all_gather(projection, 'rad', axis=0, tiled=True)]
    unnamed x15 -> x4, local copies, waits for them, and re-layouts: 27.2 us -> 3.13 us
    all_to_all x3 -> x0, starting transfers between devices: 14.1 us -> none  [the longest x1 7.47 us: per_device(): lax.all_to_all(field, 'rad', split_axis=2, concat_axis=0, tiled=True)]
    all_to_all x2 -> x0, local copies, waits for them, and re-layouts: 12.2 us -> none  [per_device(): lax.all_to_all(field, 'rad', split_axis=2, concat_axis=0, tiled=True)]
    psum x1 -> x0, blocking collectives: 6.3 us -> none  [per_device(): column = lax.psum(local_sum, 'ell')]
    pmax x1 -> x0, blocking collectives: 5.96 us -> none  [per_device(): top = lax.pmax(local_top, 'ell')]
  transfers between devices with their start and end apart: 4 -> 0, of which waited for: 3 -> 0; matrix products, arithmetic and copies ran while one was open for 15% -> 0% of each run, Pallas kernels for 0% -> 0%
where the time goes in v1:
time: 93 us; the launch traced here: 92.8 us
  Pallas kernels  84.9 us (91%)
  local copies, waits for them, and re-layouts  3.83 us (4%)
  other arithmetic  3.35 us (4%)
    pallas_call x1, Pallas kernels, by_ells(): pl.pallas_call(functools.partial(project_kernel, n, n_ell, own, depth, m_...  84.9 us
    unnamed x4, local copies, waits for them, and re-layouts  3.13 us
    transpose x1, other arithmetic, by_ells(): fp = jnp.transpose(jnp.concatenate([field, projection], axis=2), (1, 0, 2))  1.92 us

profile of v1, /device:TPU:0, one launch (start us, length us, event | category | flops | bytes accessed | tf_op | source)
XLA Modules:
  0.0 92.8 jit_solution(6764951698754989231)
XLA Ops:
  0.6 0.0 copy-start
  0.6 2.0 %copy.6 = bf16[64,32,256]{2,0,1:T(8,128)(2,1)S(1)} copy(bf16[64,32,256]{2,1,0:T(8,128)(2,1)} %param.4) | data formatting | bytes 2097152 | tf_op args[1]
  2.6 0.0 copy-done
  2.6 1.2 %copy.5 = bf16[64,32,512]{2,0,1:T(8,128)(2,1)S(1)} copy(bf16[64,32,512]{2,1,0:T(8,128)(2,1)S(1)} %copy-done) | data formatting | bytes 4194304 | tf_op args[0]
  3.8 1.9 %maximum_bitcast_fusion.fp_ref = bf16[32,64,768]{2,1,0:T(8,128)(2,1)} fusion(bf16[64,32,256]{2,0,1:T(8,128)(2,1)S(1)} %copy.6, bf16[64,32,512]{2,0,1:T(8,128)(2,1)S(1)} %copy.5), kind=kLoop, calls=%fused_computation | loop fusion | flops 6291456 | bytes 6291456 | tf_op jit(solution)/shard_map/transpose | solution.py:124
  5.7 84.9 %shard_map.50 = (f32[32,256]{1,0:T(8,128)}, f32[32,256]{1,0:T(8,128)}, f32[2,256]{1,0:T(2,128)}) custom-call(s32[32]{0:T(128)} %ell_ref.1, bf16[32,64,768]{2,1,0:T(8,128)(2,1)} %maximum_bitcast_fusion.fp_ref), custom_call_target="tpu_custom_call" | custom-call | tf_op jit(solution)/shard_map/pallas_call | solution.py:126
  90.7 0.7 constant_dynamic-slice_fusion
  91.4 1.4 %dynamic-slice_divide_fusion = (f32[32,32]{1,0:T(8,128)}, f32[32,32]{1,0:T(8,128)}) fusion(f32[32,256]{1,0:T(8,128)} %get-tuple-element.7, s32[]{:T(128)S(6)} %select_n.2, f32[32]{0:T(128)S(1)} %get-tuple-element.8, f32[32]{0:T(128)S(1)} %get-tuple-element.9, f32[32,256]{1,0:T(8,128)} %get-tuple-element.5), kind=kLoop, calls=%fused_computation.1 | loop fusion | flops 3072 | bytes 16644 | tf_op jit(solution)/shard_map/div | solution.py:155
  (1 shorter events, 0.0 us)
Async XLA Ops:
  0.6 2.0 %copy-start = (bf16[64,32,512]{2,1,0:T(8,128)(2,1)S(1)}, bf16[64,32,512]{2,1,0:T(8,128)(2,1)}, u32[]{:S(2)}) copy-start(bf16[64,32,512]{2,1,0:T(8,128)(2,1)} %param.3) | copy-start | bytes 6291460

commit v2 on v1

--- a/solution.py
+++ b/solution.py
@@ -19,8 +19,8 @@
     return peer
 
 
-def project_kernel(n, n_ell, own, depth, m_size, n_size, ell_ref, fp_ref, energy_ref, peak_ref, total_ref,
-                   held, mine, stats, mine2, totals,
+def project_kernel(n, n_ell, own, depth, m_size, n_size, ell_ref, f_ref, p_ref, share_ref, crest_ref,
+                   held_f, held_p, mine, stats, mine2, totals,
                    send_sem, recv_sem, local_sem, send2, recv2, send3, recv3):
     me = lax.axis_index("rad")
     my_ell = lax.axis_index("ell")
@@ -33,35 +33,38 @@
     rows = pl.ds(pl.multiple_of(me * depth, depth), depth)
     locals_ = []
     for e in range(own):
-        copy = pltpu.make_async_copy(fp_ref.at[me * own + e], held.at[e, rows], local_sem.at[e])
-        copy.start()
-        locals_.append(copy)
+        for i, (src, held) in enumerate(((f_ref, held_f), (p_ref, held_p))):
+            copy = pltpu.make_async_copy(src.at[me * own + e], held.at[e, rows], local_sem.at[i, e])
+            copy.start()
+            locals_.append(copy)
     pl.semaphore_wait(barrier, n - 1 + n_ell - 1)
 
-    sends = []
-    for e in range(own):
-        chunk = []
-        for s in range(n - 1, 0, -1):
-            peer = flipped(me, s, n)
-            copy = pltpu.make_async_remote_copy(
-                src_ref=fp_ref.at[peer * own + e],
-                dst_ref=held.at[e, rows],
-                send_sem=send_sem.at[e, s],
-                recv_sem=recv_sem.at[e, s],
-                device_id={"rad": peer},
-                device_id_type=MESH,
-            )
-            copy.start()
-            chunk.append(copy)
-        sends.append(chunk)
+    sends = [[] for _ in range(own)]
+    half = n // 2
+    for steps in (range(half - 1, 0, -1), range(n - 1, half - 1, -1)):
+        for e in range(own):
+            for s in steps:
+                peer = flipped(me, s, n)
+                for i, (src, held) in enumerate(((p_ref, held_p), (f_ref, held_f))):
+                    copy = pltpu.make_async_remote_copy(
+                        src_ref=src.at[peer * own + e],
+                        dst_ref=held.at[e, rows],
+                        send_sem=send_sem.at[i, e, s],
+                        recv_sem=recv_sem.at[i, e, s],
+                        device_id={"rad": peer},
+                        device_id_type=MESH,
+                    )
+                    copy.start()
+                    sends[e].append(copy)
 
     slots = lax.broadcasted_iota(jnp.int32, (m_size, n_size), 0)
     for e in range(own):
-        locals_[e].wait()
+        locals_[2 * e].wait()
+        locals_[2 * e + 1].wait()
         for copy in sends[e]:
             copy.wait_recv()
         coef = lax.dot_general(
-            held[e, :, :m_size], held[e, :, m_size:], (((0,), (0,)), ((), ())),
+            held_f[e], held_p[e], (((0,), (0,)), ((), ())),
             preferred_element_type=jnp.float32,
         )
         valid = slots < 2 * ell_ref[me * own + e] + 1
@@ -84,8 +87,6 @@
     column = jnp.zeros((1, n_size), jnp.float32)
     top = jnp.zeros((1, n_size), jnp.float32)
     for s in range(n):
-        energy_ref[s * own : (s + 1) * own, :] = every[s, :own]
-        peak_ref[s * own : (s + 1) * own, :] = every[s, own:]
         column = column + jnp.sum(every[s, :own], axis=0, keepdims=True)
         top = jnp.maximum(top, jnp.max(every[s, own:], axis=0, keepdims=True))
     mine2[0:1, :] = column
@@ -107,8 +108,11 @@
     for s in range(1, n_ell):
         column = column + both[s, 0:1]
         top = jnp.maximum(top, both[s, 1:2])
-    total_ref[0:1, :] = column
-    total_ref[1:2, :] = top
+    column = column + 1e-06
+    top = top + 1e-06
+    for s in range(n):
+        share_ref[s * own : (s + 1) * own, :] = (n * own * n_ell) * every[s, :own] / column
+        crest_ref[s * own : (s + 1) * own, :] = every[s, own:] / top
     for chunk in sends:
         for copy in chunk:
             copy.wait_send()
@@ -121,39 +125,35 @@
     depth, ells, m_size = field.shape
     n_size = projection.shape[2]
     own = ells // n
-    fp = jnp.transpose(jnp.concatenate([field, projection], axis=2), (1, 0, 2))
     vmem = pl.BlockSpec(memory_space=pltpu.VMEM)
-    energy, peak, total = pl.pallas_call(
+    share, crest = pl.pallas_call(
         functools.partial(project_kernel, n, n_ell, own, depth, m_size, n_size),
         out_shape=(
             jax.ShapeDtypeStruct((ells, n_size), jnp.float32),
             jax.ShapeDtypeStruct((ells, n_size), jnp.float32),
-            jax.ShapeDtypeStruct((2, n_size), jnp.float32),
         ),
-        in_specs=[pl.BlockSpec(memory_space=pltpu.SMEM), pl.BlockSpec(memory_space=pl.ANY)],
-        out_specs=(vmem, vmem, vmem),
+        in_specs=[pl.BlockSpec(memory_space=pltpu.SMEM)] + [pl.BlockSpec(memory_space=pl.ANY)] * 2,
+        out_specs=(vmem, vmem),
         scratch_shapes=[
-            pltpu.VMEM((own, n * depth, m_size + n_size), jnp.bfloat16),
+            pltpu.VMEM((own, n * depth, m_size), jnp.bfloat16),
+            pltpu.VMEM((own, n * depth, n_size), jnp.bfloat16),
             pltpu.VMEM((2 * own, n_size), jnp.float32),
             pltpu.VMEM((n, 2 * own, n_size), jnp.float32),
             pltpu.VMEM((2, n_size), jnp.float32),
             pltpu.VMEM((n_ell, 2, n_size), jnp.float32),
-            pltpu.SemaphoreType.DMA((own, n)),
-            pltpu.SemaphoreType.DMA((own, n)),
-            pltpu.SemaphoreType.DMA((own,)),
+            pltpu.SemaphoreType.DMA((2, own, n)),
+            pltpu.SemaphoreType.DMA((2, own, n)),
+            pltpu.SemaphoreType.DMA((2, own)),
             pltpu.SemaphoreType.DMA((n,)),
             pltpu.SemaphoreType.DMA((n,)),
             pltpu.SemaphoreType.DMA((n_ell,)),
             pltpu.SemaphoreType.DMA((n_ell,)),
         ],
         compiler_params=pltpu.CompilerParams(collective_id=0, has_side_effects=True),
-    )(ell_ids, fp)
+    )(ell_ids, jnp.transpose(field, (1, 0, 2)), jnp.transpose(projection, (1, 0, 2)))
     width = n_size // n
     start = lax.axis_index("rad") * width
-    energy, peak, total = (lax.dynamic_slice_in_dim(a, start, width, axis=1) for a in (energy, peak, total))
-    share = (ells * n_ell) * energy / (total[0:1] + 1e-06)
-    crest = peak / (total[1:2] + 1e-06)
-    return share, crest
+    return tuple(lax.dynamic_slice_in_dim(a, start, width, axis=1) for a in (share, crest))
 
 
 def by_slots(field, projection, ell_ids):

time: 93 us -> 93.9 us (level)
  local copies, waits for them, and re-layouts: 3.83 us -> 7.2 us
  other arithmetic: 3.35 us -> 0 us
    unnamed x4, local copies, waits for them, and re-layouts: 3.13 us -> 5.77 us
    transpose x1 -> x0, other arithmetic: 1.92 us -> none  [by_ells(): fp = jnp.transpose(jnp.concatenate([field, projection], axis=2), (1, 0, 2))]
    div x2 -> x0, other arithmetic: 1.43 us -> none  [by_ells(): crest = peak / (total[1:2] + 1e-06)]
where the time goes in v2:
time: 93.9 us; the launch traced here: 93.7 us
  Pallas kernels  85.8 us (91%)
  local copies, waits for them, and re-layouts  7.2 us (8%)
    pallas_call x1, Pallas kernels, by_ells(): pl.pallas_call(functools.partial(project_kernel, n, n_ell, own, depth, m_...  85.8 us
    unnamed x4, local copies, waits for them, and re-layouts  5.77 us

profile of v2, /device:TPU:0, one launch (start us, length us, event | category | flops | bytes accessed | tf_op | source)
XLA Modules:
  0.0 93.7 jit_solution(7364710392103964775)
XLA Ops:
  0.6 0.0 copy-start
  0.6 4.2 %copy.9 = bf16[64,32,512]{2,0,1:T(8,128)(2,1)} copy(bf16[64,32,512]{2,1,0:T(8,128)(2,1)} %param.3) | data formatting | bytes 4194304 | tf_op args[0]
  4.8 0.0 copy-done
  4.8 1.6 %copy.10 = bf16[64,32,256]{2,0,1:T(8,128)(2,1)} copy(bf16[64,32,256]{2,1,0:T(8,128)(2,1)S(1)} %copy-done) | data formatting | bytes 2097152 | tf_op args[1]
  6.4 85.8 %shard_map.50 = (f32[32,256]{1,0:T(8,128)}, f32[32,256]{1,0:T(8,128)}) custom-call(s32[32]{0:T(128)} %ell_ref.1, bf16[32,64,512]{2,1,0:T(8,128)(2,1)} %bitcast.6, bf16[32,64,256]{2,1,0:T(8,128)(2,1)} %bitcast.7), custom_call_target="tpu_custom_call" | custom-call | tf_op jit(solution)/shard_map/pallas_call | solution.py:129
  92.3 1.4 %constant_dynamic-slice_fusion = (f32[32,32]{1,0:T(8,128)}, f32[32,32]{1,0:T(8,128)}) fusion(f32[32,256]{1,0:T(8,128)} %get-tuple-element.5, s32[]{:T(128)S(6)} %select_n.4, f32[32,256]{1,0:T(8,128)} %get-tuple-element.4), kind=kLoop, calls=%fused_computation.2 | loop fusion | bytes 16388 | tf_op jit(solution)/shard_map/dynamic_slice | solution.py:156
Async XLA Ops:
  0.6 4.2 %copy-start = (bf16[64,32,256]{2,1,0:T(8,128)(2,1)S(1)}, bf16[64,32,256]{2,1,0:T(8,128)(2,1)}, u32[]{:S(2)}) copy-start(bf16[64,32,256]{2,1,0:T(8,128)(2,1)} %param.4) | copy-start | bytes 3145732

commit v3 on v2

--- a/solution.py
+++ b/solution.py
@@ -20,7 +20,7 @@
 
 
 def project_kernel(n, n_ell, own, depth, m_size, n_size, ell_ref, f_ref, p_ref, share_ref, crest_ref,
-                   held_f, held_p, mine, stats, mine2, totals,
+                   stage_f, stage_p, held_f, held_p, mine, stats, mine2, totals,
                    send_sem, recv_sem, local_sem, send2, recv2, send3, recv3):
     me = lax.axis_index("rad")
     my_ell = lax.axis_index("ell")
@@ -31,31 +31,37 @@
         pl.semaphore_signal(barrier, inc=1, device_id={"ell": lax.rem(my_ell + s, n_ell)}, device_id_type=MESH)
 
     rows = pl.ds(pl.multiple_of(me * depth, depth), depth)
+    pl.semaphore_wait(barrier, n - 1 + n_ell - 1)
+
+    arrays = ((p_ref, stage_p, held_p), (f_ref, stage_f, held_f))
+
+    def stage(e):
+        for src, staged, _ in arrays:
+            staged[e] = jnp.swapaxes(src[:, e * n : (e + 1) * n, :], 0, 1)
+
     locals_ = []
+    sends = [[] for _ in range(own)]
+    stage(0)
     for e in range(own):
-        for i, (src, held) in enumerate(((f_ref, held_f), (p_ref, held_p))):
-            copy = pltpu.make_async_copy(src.at[me * own + e], held.at[e, rows], local_sem.at[i, e])
+        if e + 1 < own:
+            stage(e + 1)
+        for s in range(n - 1, 0, -1):
+            peer = flipped(me, s, n)
+            for i, (_, staged, held) in enumerate(arrays):
+                copy = pltpu.make_async_remote_copy(
+                    src_ref=staged.at[e, peer],
+                    dst_ref=held.at[e, rows],
+                    send_sem=send_sem.at[i, e, s],
+                    recv_sem=recv_sem.at[i, e, s],
+                    device_id={"rad": peer},
+                    device_id_type=MESH,
+                )
+                copy.start()
+                sends[e].append(copy)
+        for i, (_, staged, held) in enumerate(arrays):
+            copy = pltpu.make_async_copy(staged.at[e, me], held.at[e, rows], local_sem.at[i, e])
             copy.start()
             locals_.append(copy)
-    pl.semaphore_wait(barrier, n - 1 + n_ell - 1)
-
-    sends = [[] for _ in range(own)]
-    half = n // 2
-    for steps in (range(half - 1, 0, -1), range(n - 1, half - 1, -1)):
-        for e in range(own):
-            for s in steps:
-                peer = flipped(me, s, n)
-                for i, (src, held) in enumerate(((p_ref, held_p), (f_ref, held_f))):
-                    copy = pltpu.make_async_remote_copy(
-                        src_ref=src.at[peer * own + e],
-                        dst_ref=held.at[e, rows],
-                        send_sem=send_sem.at[i, e, s],
-                        recv_sem=recv_sem.at[i, e, s],
-                        device_id={"rad": peer},
-                        device_id_type=MESH,
-                    )
-                    copy.start()
-                    sends[e].append(copy)
 
     slots = lax.broadcasted_iota(jnp.int32, (m_size, n_size), 0)
     for e in range(own):
@@ -67,7 +73,7 @@
             held_f[e], held_p[e], (((0,), (0,)), ((), ())),
             preferred_element_type=jnp.float32,
         )
-        valid = slots < 2 * ell_ref[me * own + e] + 1
+        valid = slots < 2 * ell_ref[e * n + me] + 1
         coef = jnp.where(valid, coef, 0.0)
         mine[e : e + 1, :] = jnp.sum(coef * coef, axis=0, keepdims=True)
         mine[own + e : own + e + 1, :] = jnp.max(jnp.abs(coef), axis=0, keepdims=True)
@@ -110,9 +116,11 @@
         top = jnp.maximum(top, both[s, 1:2])
     column = column + 1e-06
     top = top + 1e-06
-    for s in range(n):
-        share_ref[s * own : (s + 1) * own, :] = (n * own * n_ell) * every[s, :own] / column
-        crest_ref[s * own : (s + 1) * own, :] = every[s, own:] / top
+    for e in range(own):
+        for s in range(n):
+            at = slice(e * n + s, e * n + s + 1)
+            share_ref[at, :] = (n * own * n_ell) * every[s, e : e + 1] / column
+            crest_ref[at, :] = every[s, own + e : own + e + 1] / top
     for chunk in sends:
         for copy in chunk:
             copy.wait_send()
@@ -132,9 +140,11 @@
             jax.ShapeDtypeStruct((ells, n_size), jnp.float32),
             jax.ShapeDtypeStruct((ells, n_size), jnp.float32),
         ),
-        in_specs=[pl.BlockSpec(memory_space=pltpu.SMEM)] + [pl.BlockSpec(memory_space=pl.ANY)] * 2,
+        in_specs=[pl.BlockSpec(memory_space=pltpu.SMEM)] + [vmem] * 2,
         out_specs=(vmem, vmem),
         scratch_shapes=[
+            pltpu.VMEM((own, n, depth, m_size), jnp.bfloat16),
+            pltpu.VMEM((own, n, depth, n_size), jnp.bfloat16),
             pltpu.VMEM((own, n * depth, m_size), jnp.bfloat16),
             pltpu.VMEM((own, n * depth, n_size), jnp.bfloat16),
             pltpu.VMEM((2 * own, n_size), jnp.float32),
@@ -150,7 +160,7 @@
             pltpu.SemaphoreType.DMA((n_ell,)),
         ],
         compiler_params=pltpu.CompilerParams(collective_id=0, has_side_effects=True),
-    )(ell_ids, jnp.transpose(field, (1, 0, 2)), jnp.transpose(projection, (1, 0, 2)))
+    )(ell_ids, field, projection)
     width = n_size // n
     start = lax.axis_index("rad") * width
     return tuple(lax.dynamic_slice_in_dim(a, start, width, axis=1) for a in (share, crest))
@@ -186,7 +196,7 @@
 def per_device(field, projection, ell_ids):
     n = lax.axis_size("rad")
     depth, ells, _ = field.shape
-    if ells % n == 0 and n & (n - 1) == 0 and depth % 16 == 0:
+    if ells % n == 0 and n % 8 == 0 and n & (n - 1) == 0 and depth % 16 == 0:
         return by_ells(field, projection, ell_ids)
     return by_slots(field, projection, ell_ids)
 

time: 93.9 us -> 89.2 us (0.950)
  local copies, waits for them, and re-layouts: 7.2 us -> 1.43 us
  Pallas kernels: 85.8 us -> 87 us
    unnamed x4 -> x0, local copies, waits for them, and re-layouts: 5.77 us -> none
    pallas_call x1, Pallas kernels: 85.8 us -> 87 us  [by_ells(): pl.pallas_call(functools.partial(project_kernel, n, n_ell, own, depth, m_...]
where the time goes in v3:
time: 89.2 us; the launch traced here: 89.1 us
  Pallas kernels  87 us (98%)
  local copies, waits for them, and re-layouts  1.43 us (2%)
    pallas_call x1, Pallas kernels, by_ells(): pl.pallas_call(functools.partial(project_kernel, n, n_ell, own, depth, m_...  87 us

profile of v3, /device:TPU:0, one launch (start us, length us, event | category | flops | bytes accessed | tf_op | source)
XLA Modules:
  0.0 89.1 jit_solution(7121107876894215936)
XLA Ops:
  0.6 87.0 %shard_map.50 = (f32[32,256]{1,0:T(8,128)}, f32[32,256]{1,0:T(8,128)}) custom-call(s32[32]{0:T(128)} %ell_ref.1, bf16[64,32,512]{2,1,0:T(8,128)(2,1)} %f_ref.1, bf16[64,32,256]{2,1,0:T(8,128)(2,1)} %p_ref.1), custom_call_target="tpu_custom_call" | custom-call | tf_op jit(solution)/shard_map/pallas_call | solution.py:137
  87.6 1.4 %constant_dynamic-slice_fusion = (f32[32,32]{1,0:T(8,128)}, f32[32,32]{1,0:T(8,128)}) fusion(f32[32,256]{1,0:T(8,128)} %get-tuple-element.5, s32[]{:T(128)S(6)} %select_n.4, f32[32,256]{1,0:T(8,128)} %get-tuple-element.4), kind=kLoop, calls=%fused_computation | loop fusion | bytes 16388 | tf_op jit(solution)/shard_map/dynamic_slice | solution.py:166

commit v4 on v3

--- a/solution.py
+++ b/solution.py
@@ -19,9 +19,10 @@
     return peer
 
 
-def project_kernel(n, n_ell, own, depth, m_size, n_size, ell_ref, f_ref, p_ref, share_ref, crest_ref,
+def project_kernel(n, n_ell, own, depth, m_size, n_size, cut, ell_ref, f_ref, p_ref, share_ref, crest_ref,
                    stage_f, stage_p, held_f, held_p, mine, stats, mine2, totals,
-                   send_sem, recv_sem, local_sem, send2, recv2, send3, recv3):
+                   relay_f, relay_p,
+                   send_sem, recv_sem, local_sem, relay_sem, relay_send, send2, recv2, send3, recv3):
     me = lax.axis_index("rad")
     my_ell = lax.axis_index("ell")
     barrier = pltpu.get_barrier_semaphore()
@@ -30,53 +31,122 @@
     for s in range(1, n_ell):
         pl.semaphore_signal(barrier, inc=1, device_id={"ell": lax.rem(my_ell + s, n_ell)}, device_id_type=MESH)
 
+    shift, half = n_ell // 2, n // 2
+    across = flipped(me, half, n)
+    greeted = n - 1 + n_ell - 1
+    if cut < m_size:
+        pl.semaphore_signal(
+            barrier, inc=1, device_id={"rad": across, "ell": lax.rem(my_ell + shift, n_ell)}, device_id_type=MESH
+        )
+        greeted += 1
     rows = pl.ds(pl.multiple_of(me * depth, depth), depth)
-    pl.semaphore_wait(barrier, n - 1 + n_ell - 1)
-
-    arrays = ((p_ref, stage_p, held_p), (f_ref, stage_f, held_f))
-
-    def stage(e):
-        for src, staged, _ in arrays:
-            staged[e] = jnp.swapaxes(src[:, e * n : (e + 1) * n, :], 0, 1)
-
-    locals_ = []
-    sends = [[] for _ in range(own)]
-    stage(0)
-    for e in range(own):
-        if e + 1 < own:
-            stage(e + 1)
-        for s in range(n - 1, 0, -1):
+    pl.semaphore_wait(barrier, greeted)
+
+    def main(role):
+        width = cut if role == 1 else m_size
+        arrays = (
+            (p_ref, stage_p, held_p, relay_p, n_size),
+            (f_ref, stage_f, held_f, relay_f, width),
+        )
+        relayed = [(0, 0), (1, 0), (0, 1)] if role else []
+
+        def stage(e):
+            for src, staged, _, _, w in arrays:
+                staged[e, :, :, :w] = jnp.swapaxes(src[:, e * n : (e + 1) * n, :w], 0, 1)
+
+        def send(i, e, s):
+            _, staged, held, _, w = arrays[i]
             peer = flipped(me, s, n)
-            for i, (_, staged, held) in enumerate(arrays):
-                copy = pltpu.make_async_remote_copy(
-                    src_ref=staged.at[e, peer],
-                    dst_ref=held.at[e, rows],
-                    send_sem=send_sem.at[i, e, s],
-                    recv_sem=recv_sem.at[i, e, s],
-                    device_id={"rad": peer},
-                    device_id_type=MESH,
+            return pltpu.make_async_remote_copy(
+                src_ref=staged.at[e, peer, :, pl.ds(0, w)],
+                dst_ref=held.at[e, rows, pl.ds(0, w)],
+                send_sem=send_sem.at[i, e, s],
+                recv_sem=recv_sem.at[i, e, s],
+                device_id={"rad": peer},
+                device_id_type=MESH,
+            )
+
+        def to_relay(k):
+            i, e = relayed[k]
+            _, staged, _, relay, _ = arrays[i]
+            return pltpu.make_async_remote_copy(
+                src_ref=staged.at[e, across],
+                dst_ref=relay.at[e],
+                send_sem=send_sem.at[i, e, half],
+                recv_sem=relay_sem.at[k],
+                device_id={"ell": lax.rem(my_ell + shift, n_ell)},
+                device_id_type=MESH,
+            )
+
+        def from_relay(k):
+            i, e = relayed[k]
+            _, _, held, relay, _ = arrays[i]
+            return pltpu.make_async_remote_copy(
+                src_ref=relay.at[e],
+                dst_ref=held.at[e, rows],
+                send_sem=relay_send.at[k],
+                recv_sem=recv_sem.at[i, e, half],
+                device_id={"rad": across, "ell": lax.rem(my_ell + shift, n_ell)},
+                device_id_type=MESH,
+            )
+
+        locals_ = []
+        arrivals = [[] for _ in range(own)]
+        waits = []
+        stage(0)
+        for e in range(own):
+            if e + 1 < own:
+                stage(e + 1)
+            if role == 2:
+                for k, (i, at) in enumerate(relayed):
+                    if at == e:
+                        copy = to_relay(k)
+                        copy.start()
+                        waits.append(copy)
+                        arrivals[e].append(from_relay(k))
+            for s in range(n - 1, 0, -1):
+                for i in range(2):
+                    if role == 2 and s == half and (i, e) in relayed:
+                        continue
+                    copy = send(i, e, s)
+                    copy.start()
+                    waits.append(copy)
+                    arrivals[e].append(copy)
+            for i, (_, staged, held, _, w) in enumerate(arrays):
+                copy = pltpu.make_async_copy(
+                    staged.at[e, me, :, pl.ds(0, w)], held.at[e, rows, pl.ds(0, w)], local_sem.at[i, e]
                 )
                 copy.start()
-                sends[e].append(copy)
-        for i, (_, staged, held) in enumerate(arrays):
-            copy = pltpu.make_async_copy(staged.at[e, me], held.at[e, rows], local_sem.at[i, e])
-            copy.start()
-            locals_.append(copy)
-
-    slots = lax.broadcasted_iota(jnp.int32, (m_size, n_size), 0)
-    for e in range(own):
-        locals_[2 * e].wait()
-        locals_[2 * e + 1].wait()
-        for copy in sends[e]:
-            copy.wait_recv()
-        coef = lax.dot_general(
-            held_f[e], held_p[e], (((0,), (0,)), ((), ())),
-            preferred_element_type=jnp.float32,
-        )
-        valid = slots < 2 * ell_ref[e * n + me] + 1
-        coef = jnp.where(valid, coef, 0.0)
-        mine[e : e + 1, :] = jnp.sum(coef * coef, axis=0, keepdims=True)
-        mine[own + e : own + e + 1, :] = jnp.max(jnp.abs(coef), axis=0, keepdims=True)
+                locals_.append(copy)
+            if role == 1 and e == 1:
+                for k in range(len(relayed)):
+                    to_relay(k).wait_recv()
+                    copy = from_relay(k)
+                    copy.start()
+                    waits.append(copy)
+
+        slots = lax.broadcasted_iota(jnp.int32, (width, n_size), 0)
+        for e in range(own):
+            locals_[2 * e].wait()
+            locals_[2 * e + 1].wait()
+            for copy in arrivals[e]:
+                copy.wait_recv()
+            coef = lax.dot_general(
+                held_f[e, :, :width], held_p[e], (((0,), (0,)), ((), ())),
+                preferred_element_type=jnp.float32,
+            )
+            valid = slots < 2 * ell_ref[e * n + me] + 1
+            coef = jnp.where(valid, coef, 0.0)
+            mine[e : e + 1, :] = jnp.sum(coef * coef, axis=0, keepdims=True)
+            mine[own + e : own + e + 1, :] = jnp.max(jnp.abs(coef), axis=0, keepdims=True)
+        for copy in waits:
+            copy.wait_send()
+
+    if cut < m_size:
+        pl.when(my_ell < shift)(functools.partial(main, 1))
+        pl.when(my_ell >= shift)(functools.partial(main, 2))
+    else:
+        main(0)
 
     copies = []
     for s in range(n - 1, 0, -1):
@@ -121,9 +191,6 @@
             at = slice(e * n + s, e * n + s + 1)
             share_ref[at, :] = (n * own * n_ell) * every[s, e : e + 1] / column
             crest_ref[at, :] = every[s, own + e : own + e + 1] / top
-    for chunk in sends:
-        for copy in chunk:
-            copy.wait_send()
     for copy in copies + others:
         copy.wait_send()
 
@@ -133,9 +200,13 @@
     depth, ells, m_size = field.shape
     n_size = projection.shape[2]
     own = ells // n
+    most = m_size // 2 - 1 - (ells * n_ell - ells * (n_ell // 2))
+    cut = min(m_size, -(-(2 * most + 1) // 128) * 128)
+    if n_ell % 2 or own < 2 or cut < 128:
+        cut = m_size
     vmem = pl.BlockSpec(memory_space=pltpu.VMEM)
     share, crest = pl.pallas_call(
-        functools.partial(project_kernel, n, n_ell, own, depth, m_size, n_size),
+        functools.partial(project_kernel, n, n_ell, own, depth, m_size, n_size, cut),
         out_shape=(
             jax.ShapeDtypeStruct((ells, n_size), jnp.float32),
             jax.ShapeDtypeStruct((ells, n_size), jnp.float32),
@@ -151,9 +222,13 @@
             pltpu.VMEM((n, 2 * own, n_size), jnp.float32),
             pltpu.VMEM((2, n_size), jnp.float32),
             pltpu.VMEM((n_ell, 2, n_size), jnp.float32),
+            pltpu.VMEM((2, depth, m_size), jnp.bfloat16),
+            pltpu.VMEM((2, depth, n_size), jnp.bfloat16),
             pltpu.SemaphoreType.DMA((2, own, n)),
             pltpu.SemaphoreType.DMA((2, own, n)),
             pltpu.SemaphoreType.DMA((2, own)),
+            pltpu.SemaphoreType.DMA((3,)),
+            pltpu.SemaphoreType.DMA((3,)),
             pltpu.SemaphoreType.DMA((n,)),
             pltpu.SemaphoreType.DMA((n,)),
             pltpu.SemaphoreType.DMA((n_ell,)),

time: 89.2 us -> 83.8 us (0.939)
  Pallas kernels: 87 us -> 81.6 us
    pallas_call x1, Pallas kernels: 87 us -> 81.6 us  [by_ells(): pl.pallas_call(functools.partial(project_kernel, n, n_ell, own, depth, m_...]
where the time goes in v4:
time: 83.8 us; the launch traced here: 83.6 us
  Pallas kernels  81.6 us (97%)
  local copies, waits for them, and re-layouts  1.43 us (2%)
    pallas_call x1, Pallas kernels, by_ells(): pl.pallas_call(functools.partial(project_kernel, n, n_ell, own, depth, m_...  81.6 us

profile of v4, /device:TPU:0, one launch (start us, length us, event | category | flops | bytes accessed | tf_op | source)
XLA Modules:
  0.0 83.6 jit_solution(1730131355874850833)
XLA Ops:
  0.6 81.6 %shard_map.50 = (f32[32,256]{1,0:T(8,128)}, f32[32,256]{1,0:T(8,128)}) custom-call(s32[32]{0:T(128)} %ell_ref.1, bf16[64,32,512]{2,1,0:T(8,128)(2,1)} %f_ref.1, bf16[64,32,256]{2,1,0:T(8,128)(2,1)} %p_ref.1), custom_call_target="tpu_custom_call" | custom-call | tf_op jit(solution)/shard_map/pallas_call | solution.py:208
  82.2 1.4 %constant_dynamic-slice_fusion = (f32[32,32]{1,0:T(8,128)}, f32[32,32]{1,0:T(8,128)}) fusion(f32[32,256]{1,0:T(8,128)} %get-tuple-element.5, s32[]{:T(128)S(6)} %select_n.4, f32[32,256]{1,0:T(8,128)} %get-tuple-element.4), kind=kLoop, calls=%fused_computation | loop fusion | bytes 16388 | tf_op jit(solution)/shard_map/dynamic_slice | solution.py:241

commit v5 on v4

--- a/solution.py
+++ b/solution.py
@@ -40,7 +40,6 @@
         )
         greeted += 1
     rows = pl.ds(pl.multiple_of(me * depth, depth), depth)
-    pl.semaphore_wait(barrier, greeted)
 
     def main(role):
         width = cut if role == 1 else m_size
@@ -94,9 +93,10 @@
         arrivals = [[] for _ in range(own)]
         waits = []
         stage(0)
+        pl.semaphore_wait(barrier, greeted)
         for e in range(own):
-            if e + 1 < own:
-                stage(e + 1)
+            for later in range(1 if e == 1 else e + 1, min(e + 2, own) if e else 0):
+                stage(later)
             if role == 2:
                 for k, (i, at) in enumerate(relayed):
                     if at == e:
@@ -139,6 +139,52 @@
             coef = jnp.where(valid, coef, 0.0)
             mine[e : e + 1, :] = jnp.sum(coef * coef, axis=0, keepdims=True)
             mine[own + e : own + e + 1, :] = jnp.max(jnp.abs(coef), axis=0, keepdims=True)
+
+        copies = []
+        for s in range(n - 1, 0, -1):
+            copy = pltpu.make_async_remote_copy(
+                src_ref=mine, dst_ref=stats.at[me], send_sem=send2.at[s], recv_sem=recv2.at[s],
+                device_id={"rad": flipped(me, s, n)}, device_id_type=MESH,
+            )
+            copy.start()
+            copies.append(copy)
+        stats[me] = mine[...]
+        for copy in copies:
+            copy.wait_recv()
+        every = stats[...]
+        column = jnp.zeros((1, n_size), jnp.float32)
+        top = jnp.zeros((1, n_size), jnp.float32)
+        for s in range(n):
+            column = column + jnp.sum(every[s, :own], axis=0, keepdims=True)
+            top = jnp.maximum(top, jnp.max(every[s, own:], axis=0, keepdims=True))
+        mine2[0:1, :] = column
+        mine2[1:2, :] = top
+        others = []
+        for s in range(1, n_ell):
+            copy = pltpu.make_async_remote_copy(
+                src_ref=mine2, dst_ref=totals.at[my_ell], send_sem=send3.at[s], recv_sem=recv3.at[s],
+                device_id={"ell": lax.rem(my_ell + s, n_ell)}, device_id_type=MESH,
+            )
+            copy.start()
+            others.append(copy)
+        totals[my_ell] = mine2[...]
+        for copy in others:
+            copy.wait_recv()
+        both = totals[...]
+        column = both[0, 0:1]
+        top = both[0, 1:2]
+        for s in range(1, n_ell):
+            column = column + both[s, 0:1]
+            top = jnp.maximum(top, both[s, 1:2])
+        column = column + 1e-06
+        top = top + 1e-06
+        for e in range(own):
+            for s in range(n):
+                at = slice(e * n + s, e * n + s + 1)
+                share_ref[at, :] = (n * own * n_ell) * every[s, e : e + 1] / column
+                crest_ref[at, :] = every[s, own + e : own + e + 1] / top
+        for copy in copies + others:
+            copy.wait_send()
         for copy in waits:
             copy.wait_send()
 
@@ -147,52 +193,6 @@
         pl.when(my_ell >= shift)(functools.partial(main, 2))
     else:
         main(0)
-
-    copies = []
-    for s in range(n - 1, 0, -1):
-        copy = pltpu.make_async_remote_copy(
-            src_ref=mine, dst_ref=stats.at[me], send_sem=send2.at[s], recv_sem=recv2.at[s],
-            device_id={"rad": flipped(me, s, n)}, device_id_type=MESH,
-        )
-        copy.start()
-        copies.append(copy)
-    stats[me] = mine[...]
-    for copy in copies:
-        copy.wait_recv()
-    every = stats[...]
-    column = jnp.zeros((1, n_size), jnp.float32)
-    top = jnp.zeros((1, n_size), jnp.float32)
-    for s in range(n):
-        column = column + jnp.sum(every[s, :own], axis=0, keepdims=True)
-        top = jnp.maximum(top, jnp.max(every[s, own:], axis=0, keepdims=True))
-    mine2[0:1, :] = column
-    mine2[1:2, :] = top
-    others = []
-    for s in range(1, n_ell):
-        copy = pltpu.make_async_remote_copy(
-            src_ref=mine2, dst_ref=totals.at[my_ell], send_sem=send3.at[s], recv_sem=recv3.at[s],
-            device_id={"ell": lax.rem(my_ell + s, n_ell)}, device_id_type=MESH,
-        )
-        copy.start()
-        others.append(copy)
-    totals[my_ell] = mine2[...]
-    for copy in others:
-        copy.wait_recv()
-    both = totals[...]
-    column = both[0, 0:1]
-    top = both[0, 1:2]
-    for s in range(1, n_ell):
-        column = column + both[s, 0:1]
-        top = jnp.maximum(top, both[s, 1:2])
-    column = column + 1e-06
-    top = top + 1e-06
-    for e in range(own):
-        for s in range(n):
-            at = slice(e * n + s, e * n + s + 1)
-            share_ref[at, :] = (n * own * n_ell) * every[s, e : e + 1] / column
-            crest_ref[at, :] = every[s, own + e : own + e + 1] / top
-    for copy in copies + others:
-        copy.wait_send()
 
 
 def by_ells(field, projection, ell_ids):

time: 83.8 us -> 83.5 us (level)
  no operation moved by 1% of the time
where the time goes in v5:
time: 83.5 us; the launch traced here: 83.3 us
  Pallas kernels  81.2 us (97%)
  local copies, waits for them, and re-layouts  1.43 us (2%)
    pallas_call x1, Pallas kernels, by_ells(): pl.pallas_call(functools.partial(project_kernel, n, n_ell, own, depth, m_...  81.2 us

profile of v5, /device:TPU:0, one launch (start us, length us, event | category | flops | bytes accessed | tf_op | source)
XLA Modules:
  0.0 83.3 jit_solution(61106137468957484)
XLA Ops:
  0.6 81.2 %shard_map.50 = (f32[32,256]{1,0:T(8,128)}, f32[32,256]{1,0:T(8,128)}) custom-call(s32[32]{0:T(128)} %ell_ref.1, bf16[64,32,512]{2,1,0:T(8,128)(2,1)} %f_ref.1, bf16[64,32,256]{2,1,0:T(8,128)(2,1)} %p_ref.1), custom_call_target="tpu_custom_call" | custom-call | tf_op jit(solution)/shard_map/pallas_call | solution.py:208
  81.9 1.4 %constant_dynamic-slice_fusion = (f32[32,32]{1,0:T(8,128)}, f32[32,32]{1,0:T(8,128)}) fusion(f32[32,256]{1,0:T(8,128)} %get-tuple-element.5, s32[]{:T(128)S(6)} %select_n.4, f32[32,256]{1,0:T(8,128)} %get-tuple-element.4), kind=kLoop, calls=%fused_computation | loop fusion | bytes 16388 | tf_op jit(solution)/shard_map/dynamic_slice | solution.py:241

commit v6 on v5

--- a/solution.py
+++ b/solution.py
@@ -94,9 +94,25 @@
         waits = []
         stage(0)
         pl.semaphore_wait(barrier, greeted)
+        near = list(range(half - 1, 0, -1))
+        far = [half + at for pair in zip(range(half // 2, half), range(half // 2)) for at in pair]
+
+        def start(e, steps):
+            for s in steps:
+                for i in range(2):
+                    if role == 2 and s == half and (i, e) in relayed:
+                        continue
+                    copy = send(i, e, s)
+                    copy.start()
+                    waits.append(copy)
+                    arrivals[e].append(copy)
+
         for e in range(own):
-            for later in range(1 if e == 1 else e + 1, min(e + 2, own) if e else 0):
-                stage(later)
+            if e == 1:
+                for later in range(1, own):
+                    stage(later)
+                for later in range(1, own):
+                    start(later, near)
             if role == 2:
                 for k, (i, at) in enumerate(relayed):
                     if at == e:
@@ -104,14 +120,9 @@
                         copy.start()
                         waits.append(copy)
                         arrivals[e].append(from_relay(k))
-            for s in range(n - 1, 0, -1):
-                for i in range(2):
-                    if role == 2 and s == half and (i, e) in relayed:
-                        continue
-                    copy = send(i, e, s)
-                    copy.start()
-                    waits.append(copy)
-                    arrivals[e].append(copy)
+            if e == 0:
+                start(e, near)
+            start(e, far)
             for i, (_, staged, held, _, w) in enumerate(arrays):
                 copy = pltpu.make_async_copy(
                     staged.at[e, me, :, pl.ds(0, w)], held.at[e, rows, pl.ds(0, w)], local_sem.at[i, e]

time: 83.5 us -> 84 us (level)
  no operation moved by 1% of the time
where the time goes in v6:
time: 84 us; the launch traced here: 83.8 us
  Pallas kernels  81.8 us (97%)
  local copies, waits for them, and re-layouts  1.43 us (2%)
    pallas_call x1, Pallas kernels, by_ells(): pl.pallas_call(functools.partial(project_kernel, n, n_ell, own, depth, m_...  81.8 us

profile of v6, /device:TPU:0, one launch (start us, length us, event | category | flops | bytes accessed | tf_op | source)
XLA Modules:
  0.0 83.8 jit_solution(4115862617265075584)
XLA Ops:
  0.6 81.8 %shard_map.50 = (f32[32,256]{1,0:T(8,128)}, f32[32,256]{1,0:T(8,128)}) custom-call(s32[32]{0:T(128)} %ell_ref.1, bf16[64,32,512]{2,1,0:T(8,128)(2,1)} %f_ref.1, bf16[64,32,256]{2,1,0:T(8,128)(2,1)} %p_ref.1), custom_call_target="tpu_custom_call" | custom-call | tf_op jit(solution)/shard_map/pallas_call | solution.py:219
  82.4 1.4 %constant_dynamic-slice_fusion = (f32[32,32]{1,0:T(8,128)}, f32[32,32]{1,0:T(8,128)}) fusion(f32[32,256]{1,0:T(8,128)} %get-tuple-element.5, s32[]{:T(128)S(6)} %select_n.4, f32[32,256]{1,0:T(8,128)} %get-tuple-element.4), kind=kLoop, calls=%fused_computation | loop fusion | bytes 16388 | tf_op jit(solution)/shard_map/dynamic_slice | solution.py:252

commit v7 on v5

--- a/solution.py
+++ b/solution.py
@@ -19,8 +19,8 @@
     return peer
 
 
-def project_kernel(n, n_ell, own, depth, m_size, n_size, cut, ell_ref, f_ref, p_ref, share_ref, crest_ref,
-                   stage_f, stage_p, held_f, held_p, mine, stats, mine2, totals,
+def project_kernel(n, n_ell, own, depth, m_size, n_size, cut, ell_ref, f_hbm, p_hbm, share_ref, crest_ref,
+                   f_ref, p_ref, fetch_sem, stage_f, stage_p, held_f, held_p, mine, stats, mine2, totals,
                    relay_f, relay_p,
                    send_sem, recv_sem, local_sem, relay_sem, relay_send, send2, recv2, send3, recv3):
     me = lax.axis_index("rad")
@@ -40,6 +40,12 @@
         )
         greeted += 1
     rows = pl.ds(pl.multiple_of(me * depth, depth), depth)
+    fetches = [
+        pltpu.make_async_copy(src, dst, fetch_sem.at[i])
+        for i, (src, dst) in enumerate(((f_hbm, f_ref), (p_hbm, p_ref)))
+    ]
+    for copy in fetches:
+        copy.start()
 
     def main(role):
         width = cut if role == 1 else m_size
@@ -92,6 +98,8 @@
         locals_ = []
         arrivals = [[] for _ in range(own)]
         waits = []
+        for copy in fetches:
+            copy.wait()
         stage(0)
         pl.semaphore_wait(barrier, greeted)
         for e in range(own):
@@ -211,9 +219,12 @@
             jax.ShapeDtypeStruct((ells, n_size), jnp.float32),
             jax.ShapeDtypeStruct((ells, n_size), jnp.float32),
         ),
-        in_specs=[pl.BlockSpec(memory_space=pltpu.SMEM)] + [vmem] * 2,
+        in_specs=[pl.BlockSpec(memory_space=pltpu.SMEM)] + [pl.BlockSpec(memory_space=pl.ANY)] * 2,
         out_specs=(vmem, vmem),
         scratch_shapes=[
+            pltpu.VMEM(field.shape, jnp.bfloat16),
+            pltpu.VMEM(projection.shape, jnp.bfloat16),
+            pltpu.SemaphoreType.DMA((2,)),
             pltpu.VMEM((own, n, depth, m_size), jnp.bfloat16),
             pltpu.VMEM((own, n, depth, n_size), jnp.bfloat16),
             pltpu.VMEM((own, n * depth, m_size), jnp.bfloat16),

time: 83.5 us -> 82.1 us (0.983)
  Pallas kernels: 81.2 us -> 79.9 us
    pallas_call x1, Pallas kernels: 81.2 us -> 79.9 us  [by_ells(): pl.pallas_call(functools.partial(project_kernel, n, n_ell, own, depth, m_...]
where the time goes in v7:
time: 82.1 us; the launch traced here: 81.9 us
  Pallas kernels  79.9 us (97%)
  local copies, waits for them, and re-layouts  1.43 us (2%)
    pallas_call x1, Pallas kernels, by_ells(): pl.pallas_call(functools.partial(project_kernel, n, n_ell, own, depth, m_...  79.9 us

profile of v7, /device:TPU:0, one launch (start us, length us, event | category | flops | bytes accessed | tf_op | source)
XLA Modules:
  0.0 81.9 jit_solution(18230054624108719377)
XLA Ops:
  0.6 79.9 %shard_map.50 = (f32[32,256]{1,0:T(8,128)}, f32[32,256]{1,0:T(8,128)}) custom-call(s32[32]{0:T(128)} %ell_ref.1, bf16[64,32,512]{2,1,0:T(8,128)(2,1)} %f_hbm.1, bf16[64,32,256]{2,1,0:T(8,128)(2,1)} %p_hbm.1), custom_call_target="tpu_custom_call" | custom-call | tf_op jit(solution)/shard_map/pallas_call | solution.py:216
  80.5 1.4 %constant_dynamic-slice_fusion = (f32[32,32]{1,0:T(8,128)}, f32[32,32]{1,0:T(8,128)}) fusion(f32[32,256]{1,0:T(8,128)} %get-tuple-element.5, s32[]{:T(128)S(6)} %select_n.4, f32[32,256]{1,0:T(8,128)} %get-tuple-element.4), kind=kLoop, calls=%fused_computation | loop fusion | bytes 16388 | tf_op jit(solution)/shard_map/dynamic_slice | solution.py:252

commit v8 on v7

--- a/solution.py
+++ b/solution.py
@@ -112,7 +112,7 @@
                         copy.start()
                         waits.append(copy)
                         arrivals[e].append(from_relay(k))
-            for s in range(n - 1, 0, -1):
+            for s in [*range(half - 1, 0, -1), *range(n - 1, half - 1, -1)]:
                 for i in range(2):
                     if role == 2 and s == half and (i, e) in relayed:
                         continue

time: 82.1 us -> 82.3 us (level)
  no operation moved by 1% of the time
where the time goes in v8:
time: 82.3 us; the launch traced here: 82.1 us
  Pallas kernels  80 us (97%)
  local copies, waits for them, and re-layouts  1.43 us (2%)
    pallas_call x1, Pallas kernels, by_ells(): pl.pallas_call(functools.partial(project_kernel, n, n_ell, own, depth, m_...  80 us

profile of v8, /device:TPU:0, one launch (start us, length us, event | category | flops | bytes accessed | tf_op | source)
XLA Modules:
  0.0 82.1 jit_solution(13718725475640324674)
XLA Ops:
  0.6 80.0 %shard_map.50 = (f32[32,256]{1,0:T(8,128)}, f32[32,256]{1,0:T(8,128)}) custom-call(s32[32]{0:T(128)} %ell_ref.1, bf16[64,32,512]{2,1,0:T(8,128)(2,1)} %f_hbm.1, bf16[64,32,256]{2,1,0:T(8,128)(2,1)} %p_hbm.1), custom_call_target="tpu_custom_call" | custom-call | tf_op jit(solution)/shard_map/pallas_call | solution.py:216
  80.7 1.4 %constant_dynamic-slice_fusion = (f32[32,32]{1,0:T(8,128)}, f32[32,32]{1,0:T(8,128)}) fusion(f32[32,256]{1,0:T(8,128)} %get-tuple-element.5, s32[]{:T(128)S(6)} %select_n.4, f32[32,256]{1,0:T(8,128)} %get-tuple-element.4), kind=kLoop, calls=%fused_computation | loop fusion | bytes 16388 | tf_op jit(solution)/shard_map/dynamic_slice | solution.py:252
